TPU v7x, 512 devices: a whole 4x4x16 slice. The times are simulated.
512 devices in a mesh: dp: 16 (over x, y), expert: 32 (over z, core).
Axes of the slice: x: 4, y: 4, z: 16, core: 2. Of those that a mesh axis runs over, the one named last changes fastest.
Arguments:
- tokens: bfloat16 [16384, 3584], P('expert', 'dp'), may hold values from -6 to 6
- grad_out: bfloat16 [16384, 3584], P('expert', 'dp'), may hold values from -1.796875 to 1.796875
- expert_ids: int32 [16384, 8], P('expert'), may hold values from 0 to 255, as said below
- gates: float32 [16384, 8], P('expert'), may hold values from 0.25 to 2.5
- w_gate: bfloat16 [32, 3584, 1024], P('expert', 'dp'), may hold values from -0.09375 to 0.09375
- w_up: bfloat16 [32, 3584, 1024], P('expert', 'dp'), may hold values from -0.09375 to 0.09375
- w_down: bfloat16 [32, 1024, 3584], P('expert', None, 'dp'), may hold values from -0.1875 to 0.1875
Outputs:
- mixed: bfloat16 [16384, 3584], P('expert', 'dp')
- grad_tokens: bfloat16 [16384, 3584], P('expert', 'dp')
- grad_gate: bfloat16 [32, 3584, 1024], P('expert', 'dp')
- grad_up: bfloat16 [32, 3584, 1024], P('expert', 'dp')
- grad_down: bfloat16 [32, 1024, 3584], P('expert', None, 'dp')
Inputs may be any that keep to these rules, and one draw needn't show every extreme that they name: `expert_ids`: each row names 8 different experts, at most one of them below 32. Within each aligned block of 512 rows no expert below 32 is named by more than 32 rows, and one such expert, the same in every block, is named by exactly 32 rows of every block.
All inputs are finite; a program needn't handle non-finite values.
Results may differ from a plain program's by a relative error of at most 0.029.
Values may be sent and summed in bfloat16 or wider, within the bound.
A program may use at most 64 MiB of HBM per device.

v0:
```python
import jax
import jax.numpy as jnp
from jax import lax
from jax.sharding import PartitionSpec as P


def swish_gate(value):
    return value * jax.nn.sigmoid(value)


def swish_slope(value):
    logistic = jax.nn.sigmoid(value)
    return logistic * (1.0 + value * (1.0 - logistic))


def contract_rows(left, right):
    return lax.dot_general(
        left, right, (((0,), (0,)), ((), ())), preferred_element_type=jnp.float32
    )


def contract_cols(left, right):
    return lax.dot_general(
        left, right, (((1,), (1,)), ((), ())), preferred_element_type=jnp.float32
    )


def body(tokens, grad_out, expert_ids, gates, w_gate, w_up, w_down):
    experts = lax.axis_size("expert")
    tok_rows, features = tokens.shape
    capacity = tok_rows // 16
    slot_count = experts * capacity
    in_window = expert_ids < experts
    routed = jnp.any(in_window, axis=1)
    chosen = jnp.sum(jnp.where(in_window, expert_ids, 0), axis=1)
    weight_tok = jnp.sum(jnp.where(in_window, gates, jnp.zeros_like(gates)), axis=1)
    one_hot = (
        (chosen[:, None] == jnp.arange(experts, dtype=jnp.int32)[None, :]) & routed[:, None]
    ).astype(jnp.int32)
    position = jnp.sum((jnp.cumsum(one_hot, axis=0) - one_hot) * one_hot, axis=1)
    slot_index = jnp.where(routed, chosen * capacity + position, slot_count)
    source_row = jnp.full((slot_count,), tok_rows, jnp.int32)
    source_row = source_row.at[slot_index].set(jnp.arange(tok_rows, dtype=jnp.int32), mode="drop")
    scaled = (weight_tok[:, None] * grad_out.astype(jnp.float32)).astype(jnp.bfloat16)
    send_tokens = jnp.take(tokens, source_row, axis=0, mode="fill", fill_value=0).reshape(
        experts, capacity, features
    )
    send_grads = jnp.take(scaled, source_row, axis=0, mode="fill", fill_value=0).reshape(
        experts, capacity, features
    )
    arrived_tokens, arrived_grads = (
        lax.all_to_all(send_tokens, "expert", split_axis=0, concat_axis=0, tiled=True),
        lax.all_to_all(send_grads, "expert", split_axis=0, concat_axis=0, tiled=True),
    )
    expert_rows = arrived_tokens.reshape(slot_count, features)
    grad_rows_in = arrived_grads.reshape(slot_count, features)
    gate_mat = w_gate[0]
    up_mat = w_up[0]
    down_mat = w_down[0]
    part_gate = jnp.dot(expert_rows, gate_mat, preferred_element_type=jnp.float32)
    part_up = jnp.dot(expert_rows, up_mat, preferred_element_type=jnp.float32)
    gate_pre, up_pre = (
        lax.psum(part_gate.astype(jnp.bfloat16), "dp").astype(jnp.float32),
        lax.psum(part_up.astype(jnp.bfloat16), "dp").astype(jnp.float32),
    )
    full_act = (swish_gate(gate_pre) * up_pre).astype(jnp.bfloat16)
    expert_out = jnp.dot(full_act, down_mat, preferred_element_type=jnp.float32).astype(
        jnp.bfloat16
    )
    out_blocks = expert_out.reshape(experts, capacity, features)
    back_out = lax.all_to_all(out_blocks, "expert", split_axis=0, concat_axis=0, tiled=True)
    grad_down = contract_rows(full_act, grad_rows_in).astype(jnp.bfloat16)
    part_act = contract_cols(grad_rows_in, down_mat)
    grad_act = lax.psum(part_act.astype(jnp.bfloat16), "dp").astype(jnp.float32)
    grad_gate_pre = (grad_act * up_pre * swish_slope(gate_pre)).astype(jnp.bfloat16)
    grad_up_pre = (grad_act * swish_gate(gate_pre)).astype(jnp.bfloat16)
    grad_gate = contract_rows(expert_rows, grad_gate_pre).astype(jnp.bfloat16)
    grad_up = contract_rows(expert_rows, grad_up_pre).astype(jnp.bfloat16)
    row_grad = (contract_cols(grad_gate_pre, gate_mat) + contract_cols(grad_up_pre, up_mat)).astype(
        jnp.bfloat16
    )
    grad_blocks = row_grad.reshape(experts, capacity, features)
    back_grad = lax.all_to_all(grad_blocks, "expert", split_axis=0, concat_axis=0, tiled=True)
    token_out = jnp.take(
        back_out.reshape(slot_count, features), slot_index, axis=0, mode="fill", fill_value=0
    )
    mixed = (weight_tok[:, None] * token_out.astype(jnp.float32)).astype(jnp.bfloat16)
    grad_tokens = jnp.take(
        back_grad.reshape(slot_count, features), slot_index, axis=0, mode="fill", fill_value=0
    )
    return (mixed, grad_tokens, grad_gate[None], grad_up[None], grad_down[None])


def solution(mesh):
    placed = (
        P("expert", "dp"),
        P("expert", "dp"),
        P("expert", None),
        P("expert", None),
        P("expert", "dp", None),
        P("expert", "dp", None),
        P("expert", None, "dp"),
    )
    return jax.shard_map(
        body,
        mesh=mesh,
        in_specs=placed,
        out_specs=(
            P("expert", "dp"),
            P("expert", "dp"),
            P("expert", "dp", None),
            P("expert", "dp", None),
            P("expert", None, "dp"),
        ),
        check_vma=False,
    )
```

profile of v0, /device:TPU:1, one launch (start us, length us, event | category | flops | bytes accessed | tf_op | source)
XLA Modules:
  0.0 363.5 jit_solution(16019415011018475140)
XLA Ops:
  7.2 0.8 select_reduce_fusion
  8.7 1.2 reduce-window.6
  10.3 2.4 scatter_custom_fusion
  13.5 1.1 copy.21
  14.6 1.1 copy.19
  15.8 3.9 %gather_fusion.2 = bf16[1024,224]{1,0:T(8,128)(2,1)S(1)} fusion(bf16[512,224]{1,0:T(8,128)(2,1)S(1)} %multiply_convert_fusion, s32[1024]{0:T(1024)S(1)} %fusion.26), kind=kCustom, calls=%fused_computation.2.clone | custom fusion | bytes 921600 | tf_op jit(solution)/shard_map/jit(_take)/gather | solution.py:48
  19.8 3.9 %gather_fusion = bf16[1024,224]{1,0:T(8,128)(2,1)S(1)} fusion(bf16[512,224]{1,0:T(8,128)(2,1)S(1)} %copy.19, s32[1024]{0:T(1024)S(1)} %fusion.26), kind=kCustom, calls=%fused_computation.clone | custom fusion | bytes 921600 | tf_op jit(solution)/shard_map/jit(_take)/gather | solution.py:45
  23.7 1.0 broadcast_select_fusion
  24.7 50.0 %all_to_all.20 = bf16[32,32,224]{2,1,0:T(8,128)(2,1)S(1)} all-to-all(bf16[32,32,224]{2,1,0:T(8,128)(2,1)S(1)} %bitcast.73), channel_id=1, replica_groups=mesh['dp'=16,'expert'=32] {'expert'}, dimensions={0} | all-to-all | bytes 917504 | tf_op jit(solution)/shard_map/all_to_all | solution.py:52
  74.8 4.0 %all-to-all-start.2 = ((bf16[32,32,224]{2,1,0:T(8,128)(2,1)}), bf16[32,32,224]{2,1,0:T(8,128)(2,1)S(1)}, u32[]{:S(2)}, u32[]{:S(2)}) async-start(bf16[32,32,224]{2,1,0:T(8,128)(2,1)} %bitcast.12), calls=%async_computation.2 | async-start | bytes 1048576 | tf_op jit(solution)/shard_map/all_to_all | solution.py:53
  78.9 2.1 convolution_convert_fusion.1
  81.0 2.0 convolution_convert_fusion.2
  83.0 29.4 %all-to-all-done.2 = bf16[32,32,224]{2,1,0:T(8,128)(2,1)S(1)} async-done(((bf16[32,32,224]{2,1,0:T(8,128)(2,1)}), bf16[32,32,224]{2,1,0:T(8,128)(2,1)S(1)}, u32[]{:S(2)}, u32[]{:S(2)}) %all-to-all-start.2) | async-done | bytes 458784 | tf_op jit(solution)/shard_map/all_to_all | solution.py:53
  112.4 2.0 convolution_convert_fusion
  114.4 144.9 %all-reduce.3.cloned.1.call-done = (bf16[1024,1024]{1,0:T(8,128)(2,1)}, bf16[1024,1024]{1,0:T(8,128)(2,1)}, bf16[1024,1024]{1,0:T(8,128)(2,1)}) async-done(((bf16[1024,1024]{1,0:T(8,128)(2,1)}, bf16[1024,1024]{1,0:T(8,128)(2,1)}, bf16[1024,1024]{1,0:T(8,128)(2,1)}), (bf16[1024,1024]{1,0:T(8,128)(2,1)}, bf16[1024,1024]{1,0:T(8,128)(2,1)}, bf16[1024,1024]{1,0:T(8,128)(2,1)})) %all-reduce.3.cloned.1.call-update) | async-done | bytes 6291472 | tf_op jit(solution)/shard_map/psum | solution.py:64
  259.4 5.6 %fusion.3 = (bf16[1024,1024]{1,0:T(8,128)(2,1)S(1)}, bf16[1024,1024]{1,0:T(8,128)(2,1)S(1)}, bf16[1024,1024]{1,0:T(8,128)(2,1)}) fusion(bf16[1024,1024]{1,0:T(8,128)(2,1)} %get-tuple-element.19, bf16[1024,1024]{1,0:T(8,128)(2,1)} %get-tuple-element.18, bf16[1024,1024]{1,0:T(8,128)(2,1)} %get-tuple-element.17), kind=kLoop, calls=%fused_computation.14 | loop fusion | flops 18874368 | bytes 12582912 | tf_op jit(solution)/shard_map/convert_element_type | solution.py:76
  265.0 0.8 fusion.17
  266.3 0.8 fusion.9
  267.1 1.0 copy.22
  268.1 13.0 %all-to-all-start.3 = ((bf16[32,32,224]{2,1,0:T(8,128)(2,1)}), bf16[32,32,224]{2,1,0:T(8,128)(2,1)S(1)}, u32[]{:S(2)}, u32[]{:S(2)}) async-start(bf16[32,32,224]{2,1,0:T(8,128)(2,1)} %bitcast.70), calls=%async_computation.3 | async-start | bytes 1048576 | tf_op jit(solution)/shard_map/all_to_all | solution.py:83
  281.1 2.5 convolution_convert_fusion.6
  283.6 1.0 copy.20
  284.6 30.0 %all-to-all-done.3 = bf16[32,32,224]{2,1,0:T(8,128)(2,1)S(1)} async-done(((bf16[32,32,224]{2,1,0:T(8,128)(2,1)}), bf16[32,32,224]{2,1,0:T(8,128)(2,1)S(1)}, u32[]{:S(2)}, u32[]{:S(2)}) %all-to-all-start.3) | async-done | bytes 458784 | tf_op jit(solution)/shard_map/all_to_all | solution.py:83
  314.6 4.7 %all-to-all-start.1 = ((bf16[32,32,224]{2,1,0:T(8,128)(2,1)}), bf16[32,32,224]{2,1,0:T(8,128)(2,1)}, u32[]{:S(2)}, u32[]{:S(2)}) async-start(bf16[32,32,224]{2,1,0:T(8,128)(2,1)} %bitcast.69), calls=%async_computation.1 | async-start | bytes 1048576 | tf_op jit(solution)/shard_map/all_to_all | solution.py:71
  319.4 3.2 fusion.10
  322.6 1.4 fusion.11
  324.6 1.5 fusion.12
  326.0 1.9 gather_fusion.3
  328.1 0.8 copy.24
  328.9 24.0 %all-to-all-done.1 = bf16[32,32,224]{2,1,0:T(8,128)(2,1)} async-done(((bf16[32,32,224]{2,1,0:T(8,128)(2,1)}), bf16[32,32,224]{2,1,0:T(8,128)(2,1)}, u32[]{:S(2)}, u32[]{:S(2)}) %all-to-all-start.1) | async-done | bytes 458784 | tf_op jit(solution)/shard_map/all_to_all | solution.py:71
  352.9 2.7 gather_fusion.1
  355.8 0.8 copy.23
  (37 shorter events, 3.5 us)
Async XLA Ops:
  7.2 73.8 %copy-start = (bf16[1,224,1024]{2,1,0:T(8,128)(2,1)S(1)}, bf16[1,224,1024]{2,1,0:T(8,128)(2,1)}, u32[]{:S(2)}) copy-start(bf16[1,224,1024]{2,1,0:T(8,128)(2,1)} %param.15) | copy-start | bytes 1376260
  23.7 55.2 %copy-start.7 = (bf16[1,224,1024]{2,1,0:T(8,128)(2,1)S(1)}, bf16[1,224,1024]{2,1,0:T(8,128)(2,1)}, u32[]{:S(2)}) copy-start(bf16[1,224,1024]{2,1,0:T(8,128)(2,1)} %param.16) | copy-start | bytes 1376260
  74.8 8.2 %copy-start.2 = (bf16[32,32,224]{2,1,0:T(8,128)(2,1)}, bf16[32,32,224]{2,1,0:T(8,128)(2,1)S(1)}, u32[]{:S(2)}) copy-start(bf16[32,32,224]{2,1,0:T(8,128)(2,1)S(1)} %all_to_all.20) | copy-start | bytes 1376260
  74.8 37.6 %all-to-all-start.2 = ((bf16[32,32,224]{2,1,0:T(8,128)(2,1)}), bf16[32,32,224]{2,1,0:T(8,128)(2,1)S(1)}, u32[]{:S(2)}, u32[]{:S(2)}) async-start(bf16[32,32,224]{2,1,0:T(8,128)(2,1)} %bitcast.12), calls=%async_computation.2 | async-start | bytes 1048576 | tf_op jit(solution)/shard_map/all_to_all | solution.py:53
  78.8 180.5 %all-reduce.3.cloned.1.call-start = ((), (), s32[]{:S(2)}) async-start(), calls=%async_computation.4 | async-start | bytes 12582912 | tf_op jit(solution)/shard_map/psum | solution.py:64
  81.0 31.4 %copy-start.8 = (bf16[1,1024,224]{1,2,0:T(8,128)(2,1)S(1)}, bf16[1,1024,224]{1,2,0:T(8,128)(2,1)}, u32[]{:S(2)}) copy-start(bf16[1,1024,224]{1,2,0:T(8,128)(2,1)} %param.17) | copy-start | bytes 1376260
  112.4 2.0 copy-start.4
  265.0 1.3 copy-start.1
  268.1 46.5 %all-to-all-start.3 = ((bf16[32,32,224]{2,1,0:T(8,128)(2,1)}), bf16[32,32,224]{2,1,0:T(8,128)(2,1)S(1)}, u32[]{:S(2)}, u32[]{:S(2)}) async-start(bf16[32,32,224]{2,1,0:T(8,128)(2,1)} %bitcast.70), calls=%async_computation.3 | async-start | bytes 1048576 | tf_op jit(solution)/shard_map/all_to_all | solution.py:83
  314.6 38.3 %all-to-all-start.1 = ((bf16[32,32,224]{2,1,0:T(8,128)(2,1)}), bf16[32,32,224]{2,1,0:T(8,128)(2,1)}, u32[]{:S(2)}, u32[]{:S(2)}) async-start(bf16[32,32,224]{2,1,0:T(8,128)(2,1)} %bitcast.69), calls=%async_computation.1 | async-start | bytes 1048576 | tf_op jit(solution)/shard_map/all_to_all | solution.py:71
  319.3 3.3 copy-start.3
  322.6 1.4 copy-start.5
  322.6 1.9 copy-start.6
Sparse Core Ops, SparseCore 0:
  114.5 144.7 all-reduce.2
where the time goes:
time: 364 us; the launch traced here: 363 us
  waiting for transfers between devices  228 us (63%)
  blocking collectives  50 us (14%)
  local copies, waits for them, and re-layouts  22 us (6%)
  starting transfers between devices  21.8 us (6%)
  matrix products  16.2 us (4%)
  between operations  14.3 us (4%)
  other arithmetic  10.7 us (3%)
    psum x1, waiting for transfers between devices, body(): lax.psum(part_up.astype(jnp.bfloat16), 'dp').astype(jnp.float32)  145 us
    all_to_all x1, blocking collectives, body(): lax.all_to_all(send_tokens, 'expert', split_axis=0, concat_axis=0, tiled=...  50 us
    all_to_all x1, waiting for transfers between devices, body(): lax.all_to_all(grad_blocks, 'expert', split_axis=0, concat_axis=0, tiled=...  30 us
    all_to_all x1, waiting for transfers between devices, body(): lax.all_to_all(send_grads, 'expert', split_axis=0, concat_axis=0, tiled=T...  29.4 us
    all_to_all x1, waiting for transfers between devices, body(): lax.all_to_all(out_blocks, 'expert', split_axis=0, concat_axis=0, tiled=T...  24 us
    all_to_all x1, starting transfers between devices, body(): lax.all_to_all(grad_blocks, 'expert', split_axis=0, concat_axis=0, tiled=...  13 us
  transfers between devices with their start and end apart: 4, of which 4 were waited for; matrix products, arithmetic and copies ran while one was open for 5% of the time, Pallas kernels for 0%

commit v1 on v0

--- a/solution.py
+++ b/solution.py
@@ -61,7 +61,7 @@
     part_up = jnp.dot(expert_rows, up_mat, preferred_element_type=jnp.float32)
     gate_pre, up_pre = (
         lax.psum(part_gate.astype(jnp.bfloat16), "dp").astype(jnp.float32),
-        lax.psum(part_up.astype(jnp.bfloat16), "dp").astype(jnp.float32),
+        jnp.sum(lax.all_gather(part_up.astype(jnp.bfloat16), "dp"), axis=0).astype(jnp.float32),
     )
     full_act = (swish_gate(gate_pre) * up_pre).astype(jnp.bfloat16)
     expert_out = jnp.dot(full_act, down_mat, preferred_element_type=jnp.float32).astype(

time: 364 us -> 523 us (1.44)
  waiting for transfers between devices: 228 us -> 374 us
  other arithmetic: 10.7 us -> 23.7 us
    all_gather x0 -> x1, waiting for transfers between devices: none -> 164 us  [body(): lax.all_gather(part_up.astype(jnp.bfloat16), 'dp')]
    psum x1, waiting for transfers between devices: 145 us -> 124 us  [body(): lax.psum(part_gate.astype(jnp.bfloat16), 'dp').astype(jnp.float32)]
    reduce_sum x0 -> x1, other arithmetic: none -> 13 us  [body(): jnp.sum(lax.all_gather(part_up.astype(jnp.bfloat16), 'dp'), axis=0)]
  transfers between devices with their start and end apart: 4 -> 5, of which waited for: 4 -> 5; matrix products, arithmetic and copies ran while one was open for 5% -> 6% of each run, Pallas kernels for 0% -> 0%
where the time goes in v1:
time: 523 us
  waiting for transfers between devices  374 us (72%)
  blocking collectives  50 us (10%)
  other arithmetic  23.7 us (5%)
  local copies, waits for them, and re-layouts  22.1 us (4%)
  starting transfers between devices  22.1 us (4%)
  matrix products  16.2 us (3%)
  between operations  14.3 us (3%)
    all_gather x1, waiting for transfers between devices, body(): lax.all_gather(part_up.astype(jnp.bfloat16), 'dp')  164 us
    psum x1, waiting for transfers between devices, body(): lax.psum(part_gate.astype(jnp.bfloat16), 'dp').astype(jnp.float32)  124 us
    all_to_all x1, blocking collectives, body(): lax.all_to_all(send_tokens, 'expert', split_axis=0, concat_axis=0, tiled=...  50 us
    all_to_all x1, waiting for transfers between devices, body(): lax.all_to_all(send_grads, 'expert', split_axis=0, concat_axis=0, tiled=T...  31.5 us
    all_to_all x1, waiting for transfers between devices, body(): lax.all_to_all(grad_blocks, 'expert', split_axis=0, concat_axis=0, tiled=...  30 us
    all_to_all x1, waiting for transfers between devices, body(): lax.all_to_all(out_blocks, 'expert', split_axis=0, concat_axis=0, tiled=T...  24 us
    all_to_all x1, starting transfers between devices, body(): lax.all_to_all(grad_blocks, 'expert', split_axis=0, concat_axis=0, tiled=...  13.2 us
    reduce_sum x1, other arithmetic, body(): jnp.sum(lax.all_gather(part_up.astype(jnp.bfloat16), 'dp'), axis=0)  13 us
  transfers between devices with their start and end apart: 5, of which 5 were waited for; matrix products, arithmetic and copies ran while one was open for 6% of the time, Pallas kernels for 0%

profile of v1, /device:TPU:1, one launch (start us, length us, event | category | flops | bytes accessed | tf_op | source)
XLA Modules:
  0.0 522.5 jit_solution(9994099560127778587)
XLA Ops:
  8.8 1.2 reduce-window.6
  10.3 2.4 scatter_custom_fusion
  13.6 1.1 copy.19
  14.7 1.1 copy.21
  15.7 3.9 gather_fusion
  19.8 3.9 gather_fusion.2
  23.8 1.0 broadcast_select_fusion
  24.8 50.0 %all_to_all.20 = bf16[32,32,224]{2,1,0:T(8,128)(2,1)S(1)} all-to-all(bf16[32,32,224]{2,1,0:T(8,128)(2,1)S(1)} %bitcast.76), channel_id=1, replica_groups=mesh['dp'=16,'expert'=32] {'expert'}, dimensions={0} | all-to-all | bytes 917504 | tf_op jit(solution)/shard_map/all_to_all | solution.py:52
  74.9 2.0 convolution_convert_fusion.1
  76.9 4.2 all-to-all-start.2
  81.2 2.0 convolution_convert_fusion.2
  83.2 31.5 %all-to-all-done.2 = bf16[32,32,224]{2,1,0:T(8,128)(2,1)S(1)} async-done(((bf16[32,32,224]{2,1,0:T(8,128)(2,1)}), bf16[32,32,224]{2,1,0:T(8,128)(2,1)S(1)}, u32[]{:S(2)}, u32[]{:S(2)}) %all-to-all-start.2) | async-done | bytes 458784 | tf_op jit(solution)/shard_map/all_to_all | solution.py:53
  114.6 2.1 convolution_convert_fusion
  116.7 164.0 %all-gather.3.cloned.1.call-done = bf16[16384,1024]{1,0:T(8,128)(2,1)} async-done(((bf16[1024,1024]{1,0:T(8,128)(2,1)}), bf16[16384,1024]{1,0:T(8,128)(2,1)}) %all-gather.3.cloned.1.call-update) | async-done | bytes 33554448 | tf_op jit(solution)/shard_map/all_gather | solution.py:64
  280.8 13.0 %reduce_sum.42 = bf16[1024,1024]{1,0:T(8,128)(2,1)} reduce(bf16[16,1024,1024]{2,1,0:T(8,128)(2,1)} %bitcast.66, bf16[]{:T(256)} %constant.14.clone.1), dimensions={0}, to_apply=%region_8.10 | reduce | flops 15728640 | bytes 35651584 | tf_op jit(solution)/shard_map/reduce_sum | solution.py:64
  293.8 124.5 %all-reduce.3.cloned.1.call-done = (bf16[1024,1024]{1,0:T(8,128)(2,1)}, bf16[1024,1024]{1,0:T(8,128)(2,1)}) async-done(((bf16[1024,1024]{1,0:T(8,128)(2,1)}, bf16[1024,1024]{1,0:T(8,128)(2,1)}), (bf16[1024,1024]{1,0:T(8,128)(2,1)}, bf16[1024,1024]{1,0:T(8,128)(2,1)})) %all-reduce.3.cloned.1.call-update) | async-done | bytes 4194320 | tf_op jit(solution)/shard_map/psum | solution.py:63
  418.3 5.6 %fusion.3 = (bf16[1024,1024]{1,0:T(8,128)(2,1)S(1)}, bf16[1024,1024]{1,0:T(8,128)(2,1)S(1)}, bf16[1024,1024]{1,0:T(8,128)(2,1)}) fusion(bf16[1024,1024]{1,0:T(8,128)(2,1)} %get-tuple-element.18, bf16[1024,1024]{1,0:T(8,128)(2,1)} %get-tuple-element.17, bf16[1024,1024]{1,0:T(8,128)(2,1)} %reduce_sum.42), kind=kLoop, calls=%fused_computation.14 | loop fusion | flops 18874368 | bytes 12582912 | tf_op jit(solution)/shard_map/convert_element_type | solution.py:76
  425.2 0.8 fusion.9
  426.0 1.0 copy.22
  427.0 13.2 %all-to-all-start.3 = ((bf16[32,32,224]{2,1,0:T(8,128)(2,1)}), bf16[32,32,224]{2,1,0:T(8,128)(2,1)S(1)}, u32[]{:S(2)}, u32[]{:S(2)}) async-start(bf16[32,32,224]{2,1,0:T(8,128)(2,1)} %bitcast.73), calls=%async_computation.3 | async-start | bytes 1048576 | tf_op jit(solution)/shard_map/all_to_all | solution.py:83
  440.2 2.5 convolution_convert_fusion.6
  442.6 1.0 copy.20
  443.7 30.0 %all-to-all-done.3 = bf16[32,32,224]{2,1,0:T(8,128)(2,1)S(1)} async-done(((bf16[32,32,224]{2,1,0:T(8,128)(2,1)}), bf16[32,32,224]{2,1,0:T(8,128)(2,1)S(1)}, u32[]{:S(2)}, u32[]{:S(2)}) %all-to-all-start.3) | async-done | bytes 458784 | tf_op jit(solution)/shard_map/all_to_all | solution.py:83
  473.7 4.7 all-to-all-start.1
  478.4 3.2 fusion.11
  481.7 1.4 fusion.10
  483.6 1.5 fusion.12
  485.1 1.9 gather_fusion.3
  487.2 0.8 copy.24
  488.0 24.0 %all-to-all-done.1 = bf16[32,32,224]{2,1,0:T(8,128)(2,1)} async-done(((bf16[32,32,224]{2,1,0:T(8,128)(2,1)}), bf16[32,32,224]{2,1,0:T(8,128)(2,1)}, u32[]{:S(2)}, u32[]{:S(2)}) %all-to-all-start.1) | async-done | bytes 458784 | tf_op jit(solution)/shard_map/all_to_all | solution.py:71
  512.0 2.7 gather_fusion.1
  514.9 0.8 copy.23
  (41 shorter events, 5.2 us)
Async XLA Ops:
  7.2 74.0 %copy-start = (bf16[1,224,1024]{2,1,0:T(8,128)(2,1)S(1)}, bf16[1,224,1024]{2,1,0:T(8,128)(2,1)}, u32[]{:S(2)}) copy-start(bf16[1,224,1024]{2,1,0:T(8,128)(2,1)} %param.15) | copy-start | bytes 1376260
  7.2 273.6 %all-gather.3.cloned.1.call-start = ((), (), s32[]{:S(2)}) async-start(), calls=%async_computation.4 | async-start | bytes 35651584 | tf_op jit(solution)/shard_map/all_gather | solution.py:64
  23.8 51.1 %copy-start.7 = (bf16[1,224,1024]{2,1,0:T(8,128)(2,1)S(1)}, bf16[1,224,1024]{2,1,0:T(8,128)(2,1)}, u32[]{:S(2)}) copy-start(bf16[1,224,1024]{2,1,0:T(8,128)(2,1)} %param.16) | copy-start | bytes 1376260
  74.9 6.3 %copy-start.2 = (bf16[32,32,224]{2,1,0:T(8,128)(2,1)}, bf16[32,32,224]{2,1,0:T(8,128)(2,1)S(1)}, u32[]{:S(2)}) copy-start(bf16[32,32,224]{2,1,0:T(8,128)(2,1)S(1)} %all_to_all.20) | copy-start | bytes 1376260
  76.9 37.7 %copy-start.8 = (bf16[1,1024,224]{1,2,0:T(8,128)(2,1)S(1)}, bf16[1,1024,224]{1,2,0:T(8,128)(2,1)}, u32[]{:S(2)}) copy-start(bf16[1,1024,224]{1,2,0:T(8,128)(2,1)} %param.17) | copy-start | bytes 1376260
  76.9 37.7 %all-to-all-start.2 = ((bf16[32,32,224]{2,1,0:T(8,128)(2,1)}), bf16[32,32,224]{2,1,0:T(8,128)(2,1)S(1)}, u32[]{:S(2)}, u32[]{:S(2)}) async-start(bf16[32,32,224]{2,1,0:T(8,128)(2,1)} %bitcast.13), calls=%async_computation.2 | async-start | bytes 1048576 | tf_op jit(solution)/shard_map/all_to_all | solution.py:53
  81.1 337.2 %all-reduce.3.cloned.1.call-start = ((), (), s32[]{:S(2)}) async-start(), calls=%async_computation.5 | async-start | bytes 8388608 | tf_op jit(solution)/shard_map/psum | solution.py:63
  114.6 2.1 copy-start.4
  423.8 1.4 copy-start.1
  427.0 46.7 %all-to-all-start.3 = ((bf16[32,32,224]{2,1,0:T(8,128)(2,1)}), bf16[32,32,224]{2,1,0:T(8,128)(2,1)S(1)}, u32[]{:S(2)}, u32[]{:S(2)}) async-start(bf16[32,32,224]{2,1,0:T(8,128)(2,1)} %bitcast.73), calls=%async_computation.3 | async-start | bytes 1048576 | tf_op jit(solution)/shard_map/all_to_all | solution.py:83
  473.7 38.3 %all-to-all-start.1 = ((bf16[32,32,224]{2,1,0:T(8,128)(2,1)}), bf16[32,32,224]{2,1,0:T(8,128)(2,1)}, u32[]{:S(2)}, u32[]{:S(2)}) async-start(bf16[32,32,224]{2,1,0:T(8,128)(2,1)} %bitcast.72), calls=%async_computation.1 | async-start | bytes 1048576 | tf_op jit(solution)/shard_map/all_to_all | solution.py:71
  478.4 3.3 copy-start.3
  481.7 1.4 copy-start.5
  481.7 1.9 copy-start.6
Sparse Core Ops, SparseCore 0:
  77.0 203.7 all-gather.2
  284.2 134.0 all-reduce.2
